TPU v7x, 256 devices: a whole 4x4x8 slice. The times are simulated.
256 devices in a mesh: tok: 8 (over z_lo, x), feat: 32 (over z_hi, y, core).
Axes of the slice: x: 4, y: 4, z: 8 (z_hi: 4, z_lo: 2; z = z_hi * 2 + z_lo), core: 2. Of those that a mesh axis runs over, the one named last changes fastest.
Arguments:
- features: bfloat16 [8192, 16384], P('tok', 'feat'), may hold values from -6 to 6
- kernel: bfloat16 [16384, 256], P('feat'), may hold values from -6 to 6
- mask: int32 [16384, 256], P('feat'), may hold values 0 or 1
- inverse: float32 [16384, 16384], P('tok', 'feat'), may hold values from -1 to 2, as said below
- penalty: float32 [3], replicated, may hold values from 0.3 to 3
Outputs:
- pruned: bfloat16 [16384, 256], P('feat')
- applied: bfloat16 [256, 8192], P('feat', 'tok')
Inputs may be any that keep to these rules, and one draw needn't show every extreme that they name: inverse is exactly symmetric.
All inputs are finite; a program needn't handle non-finite values. No bound on the sum of `mask` on one device may be relied on, other than what follows from the above.
Results may differ from a plain program's by a relative error of at most 0.0048.
Values sent between devices are 32-bit elements; how exact they have to be, the bound alone decides.
No kernel may reach another device: no remote copies, remote signals or barrier semaphores. Data moves between devices by JAX's collectives and lax.ppermute only.
A program may use at most 64 MiB of HBM per device.

v0:
```python
import math
import jax
import jax.numpy as jnp
from jax import lax
from jax.sharding import PartitionSpec as P


def broadcast(value, axis, source):
    kept = jnp.where(lax.axis_index(axis) == source, value, 0).astype(value.dtype)
    return lax.psum(kept, axis)


def per_device(features, kernel, mask, inverse, penalty):
    n_tok = lax.axis_size("tok")
    n_feat = lax.axis_size("feat")
    width = features.shape[1] * n_feat
    tokens = features.shape[0] * n_tok
    scale = 1.0 / math.sqrt(width)
    block = kernel.shape[0]
    ratio = n_feat // n_tok
    partial_value = jnp.dot(features, kernel, preferred_element_type=jnp.float32)
    targets = (lax.psum(partial_value, "feat") * scale).astype(jnp.bfloat16)
    side_part = lax.dot_general(
        features, targets, (((0,), (0,)), ((), ())), preferred_element_type=jnp.float32
    )
    sides = lax.psum(side_part, "tok") * (math.sqrt(width) / tokens)
    keeps = mask.astype(jnp.float32)
    slab = keeps * kernel.astype(jnp.float32)
    dual = jnp.zeros(slab.shape, jnp.float32)
    feat_index = lax.axis_index("feat")
    for step in range(penalty.shape[0]):
        rhs = sides + penalty[step] * (slab - dual)
        part = jnp.dot(
            inverse, rhs, precision=lax.Precision.HIGHEST, preferred_element_type=jnp.float32
        )
        total = lax.psum(part, "feat")
        offset = feat_index % ratio * block
        own_rows = lax.dynamic_slice_in_dim(total, offset, block, 0)
        solved = broadcast(own_rows, "tok", feat_index // ratio)
        slab = keeps * (solved + dual)
        dual = dual + solved - slab
    pruned = slab.astype(jnp.bfloat16)
    term = lax.dot_general(
        pruned, features, (((0,), (1,)), ((), ())), preferred_element_type=jnp.float32
    )
    applied = lax.psum_scatter(term * scale, "feat", scatter_dimension=0, tiled=True)
    return (pruned, applied.astype(jnp.bfloat16))


def solution(mesh):
    return jax.shard_map(
        per_device,
        mesh=mesh,
        in_specs=(P("tok", "feat"), P("feat", None), P("feat", None), P("tok", "feat"), P()),
        out_specs=(P("feat", None), P("feat", "tok")),
        check_vma=False,
    )
```

profile of v0, /device:TPU:2, one launch (start us, length us, event | category | flops | bytes accessed | tf_op | source)
XLA Modules:
  0.0 1635.1 jit_solution(14518243554215195061)
XLA Ops:
  7.2 0.0 copy-start
  7.2 0.0 all-reduce.9.cloned.1.call-start
  7.2 1.2 copy-done
  8.4 2.4 fusion.32
  10.8 0.0 copy-start.4
  10.8 0.0 all-reduce.9.cloned.1.call-update
  10.8 0.0 copy-start.5
  10.8 0.0 copy-start.6
  10.9 0.0 all-reduce.11.cloned.1.call-start
  10.9 292.3 %all-reduce.9.cloned.1.call-done = f32[1024,256]{1,0:T(8,128)} async-done(((f32[1024,256]{1,0:T(8,128)}), f32[1024,256]{1,0:T(8,128)}) %all-reduce.9.cloned.1.call-update) | async-done | bytes 1048592 | tf_op jit(solution)/shard_map/psum | solution.py:22
  303.2 2.5 convolution_bitcast_fusion.3
  305.7 0.0 all-reduce.11.cloned.1.call-update
  305.7 0.0 all-reduce.13.cloned.1.call-start
  305.8 0.0 copy-done.4
  305.8 0.1 copy.8
  305.9 0.0 copy-done.5
  305.9 0.2 copy.7
  306.1 0.0 copy-done.6
  306.2 0.7 fusion.31
  306.8 76.9 %all-reduce.11.cloned.1.call-done = f32[512,256]{0,1:T(8,128)} async-done(((f32[512,256]{0,1:T(8,128)}), f32[512,256]{0,1:T(8,128)}) %all-reduce.11.cloned.1.call-update) | async-done | bytes 524304 | tf_op jit(solution)/shard_map/psum | solution.py:26
  383.7 8.0 convolution_bitcast_fusion.2
  391.7 0.0 copy-start.2
  391.7 0.0 all-reduce.13.cloned.1.call-update
  391.7 0.0 all-reduce.15.cloned.1.call-start
  391.8 295.3 %all-reduce.13.cloned.1.call-done = f32[2048,256]{0,1:T(8,128)} async-done(((f32[2048,256]{0,1:T(8,128)}), f32[2048,256]{0,1:T(8,128)}) %all-reduce.13.cloned.1.call-update) | async-done | bytes 2097168 | tf_op jit(solution)/shard_map/psum | solution.py:36
  687.1 1.9 dynamic-slice_select_fusion.2
  689.0 0.0 all-reduce.15.cloned.1.call-update
  689.0 0.0 all-reduce.17.cloned.1.call-start
  689.1 77.5 %all-reduce.15.cloned.1.call-done = f32[512,256]{0,1:T(8,128)} async-done(((f32[512,256]{0,1:T(8,128)}), f32[512,256]{0,1:T(8,128)}) %all-reduce.15.cloned.1.call-update) | async-done | bytes 524304 | tf_op jit(solution)/shard_map/psum | solution.py:10
  766.5 0.0 copy-done.2
  766.5 8.1 convolution_bitcast_fusion.1
  774.6 0.0 copy-start.1
  774.6 0.0 all-reduce.17.cloned.1.call-update
  774.6 0.0 all-reduce.19.cloned.1.call-start
  774.7 295.2 %all-reduce.17.cloned.1.call-done = f32[2048,256]{0,1:T(8,128)} async-done(((f32[2048,256]{0,1:T(8,128)}), f32[2048,256]{0,1:T(8,128)}) %all-reduce.17.cloned.1.call-update) | async-done | bytes 2097168 | tf_op jit(solution)/shard_map/psum | solution.py:36
  1069.9 1.9 dynamic-slice_select_fusion.1
  1071.8 0.0 all-reduce.19.cloned.1.call-update
  1071.8 0.2 all-reduce.21.cloned.1.call-start
  1072.0 77.3 %all-reduce.19.cloned.1.call-done = f32[512,256]{0,1:T(8,128)} async-done(((f32[512,256]{0,1:T(8,128)}), f32[512,256]{0,1:T(8,128)}) %all-reduce.19.cloned.1.call-update) | async-done | bytes 524304 | tf_op jit(solution)/shard_map/psum | solution.py:10
  1149.3 0.0 copy-done.1
  1149.3 8.1 convolution_bitcast_fusion
  1157.4 0.0 copy-start.3
  1157.4 0.0 all-reduce.21.cloned.1.call-update
  1157.4 0.0 all-reduce.23.cloned.1.call-start
  1157.5 295.3 %all-reduce.21.cloned.1.call-done = f32[2048,256]{0,1:T(8,128)} async-done(((f32[2048,256]{0,1:T(8,128)}), f32[2048,256]{0,1:T(8,128)}) %all-reduce.21.cloned.1.call-update) | async-done | bytes 2097168 | tf_op jit(solution)/shard_map/psum | solution.py:36
  1452.8 1.9 dynamic-slice_select_fusion
  1454.7 0.0 all-reduce.23.cloned.1.call-update
  1454.7 0.0 reduce-scatter.2.cloned.1.call-start
  1454.7 77.6 %all-reduce.23.cloned.1.call-done = f32[512,256]{0,1:T(8,128)} async-done(((f32[512,256]{0,1:T(8,128)}), f32[512,256]{0,1:T(8,128)}) %all-reduce.23.cloned.1.call-update) | async-done | bytes 524304 | tf_op jit(solution)/shard_map/psum | solution.py:10
  1532.3 0.0 copy-done.3
  1532.3 1.3 multiply_convert_fusion.2
  1533.6 1.4 convolution_multiply_fusion
  1535.1 0.0 reduce-scatter.2.cloned.1.call-update
  1535.1 0.8 copy.9
  1536.0 91.2 %reduce-scatter.2.cloned.1.call-done = f32[8,1024]{1,0:T(8,128)} async-done(((f32[256,1024]{1,0:T(8,128)}), f32[8,1024]{1,0:T(8,128)}) %reduce-scatter.2.cloned.1.call-update) | async-done | bytes 32784 | tf_op jit(solution)/shard_map/reduce_scatter | solution.py:46
  1627.2 1.4 convert_element_type.23
Async XLA Ops:
  7.2 1.2 copy-start
  7.2 296.0 %all-reduce.9.cloned.1.call-start = ((), (), s32[]{:S(2)}) async-start(), calls=%async_computation.1 | async-start | bytes 2097152 | tf_op jit(solution)/shard_map/psum | solution.py:22
  10.8 295.0 %copy-start.4 = (bf16[512,256]{1,0:T(8,128)(2,1)S(1)}, bf16[512,256]{1,0:T(8,128)(2,1)}, u32[]{:S(2)}) copy-start(bf16[512,256]{1,0:T(8,128)(2,1)} %param.6) | copy-start | bytes 786436
  10.8 295.1 %copy-start.5 = (s32[512,256]{1,0:T(8,128)S(1)}, s32[512,256]{1,0:T(8,128)}, u32[]{:S(2)}) copy-start(s32[512,256]{1,0:T(8,128)} %param.7) | copy-start | bytes 1572868
  10.8 295.3 %copy-start.6 = (f32[3]{0:T(128)S(1)}, f32[3]{0:T(128)}, u32[]{:S(2)}) copy-start(f32[3]{0:T(128)} %param.9) | copy-start | bytes 40
  10.9 372.8 %all-reduce.11.cloned.1.call-start = ((), (), s32[]{:S(2)}) async-start(), calls=%async_computation.2 | async-start | bytes 1048576 | tf_op jit(solution)/shard_map/psum | solution.py:26
  305.7 381.4 %all-reduce.13.cloned.1.call-start = ((), (), s32[]{:S(2)}) async-start(), calls=%async_computation.3 | async-start | bytes 4194304 | tf_op jit(solution)/shard_map/psum | solution.py:36
  391.7 374.8 %copy-start.2 = (f32[512,256]{0,1:T(8,128)S(1)}, f32[512,256]{0,1:T(8,128)}, u32[]{:S(2)}) copy-start(f32[512,256]{0,1:T(8,128)} %all-reduce.11.cloned.1.call-done) | copy-start | bytes 1572868
  391.7 374.8 %all-reduce.15.cloned.1.call-start = ((), (), s32[]{:S(2)}) async-start(), calls=%async_computation.4 | async-start | bytes 1048576 | tf_op jit(solution)/shard_map/psum | solution.py:10
  689.0 380.9 %all-reduce.17.cloned.1.call-start = ((), (), s32[]{:S(2)}) async-start(), calls=%async_computation.5 | async-start | bytes 4194304 | tf_op jit(solution)/shard_map/psum | solution.py:36
  774.6 374.7 %copy-start.1 = (f32[512,256]{0,1:T(8,128)S(1)}, f32[512,256]{0,1:T(8,128)}, u32[]{:S(2)}) copy-start(f32[512,256]{0,1:T(8,128)} %all-reduce.15.cloned.1.call-done) | copy-start | bytes 1572868
  774.6 374.7 %all-reduce.19.cloned.1.call-start = ((), (), s32[]{:S(2)}) async-start(), calls=%async_computation.6 | async-start | bytes 1048576 | tf_op jit(solution)/shard_map/psum | solution.py:10
  1071.8 381.0 %all-reduce.21.cloned.1.call-start = ((), (), s32[]{:S(2)}) async-start(), calls=%async_computation.7 | async-start | bytes 4194304 | tf_op jit(solution)/shard_map/psum | solution.py:36
  1157.4 375.0 %copy-start.3 = (f32[512,256]{0,1:T(8,128)S(1)}, f32[512,256]{0,1:T(8,128)}, u32[]{:S(2)}) copy-start(f32[512,256]{0,1:T(8,128)} %all-reduce.19.cloned.1.call-done) | copy-start | bytes 1572868
  1157.4 374.9 %all-reduce.23.cloned.1.call-start = ((), (), s32[]{:S(2)}) async-start(), calls=%async_computation.8 | async-start | bytes 1048576 | tf_op jit(solution)/shard_map/psum | solution.py:10
  1454.7 172.5 %reduce-scatter.2.cloned.1.call-start = ((), (), s32[]{:S(2)}) async-start(), calls=%async_computation.9 | async-start | bytes 1081344 | tf_op jit(solution)/shard_map/reduce_scatter | solution.py:46
Sparse Core Ops, SparseCore 0:
  11.0 292.1 all-reduce.8
  305.8 77.8 all-reduce.10
  391.9 295.2 all-reduce.12
  689.6 76.8 all-reduce.14
  774.7 295.1 all-reduce.16
  1072.4 76.8 all-reduce.18
  1157.5 295.2 all-reduce.20
  1455.4 76.8 all-reduce.22
  1536.1 90.9 reduce-scatter.1
where the time goes:
time: 1640 us
  waiting for transfers between devices  1580 us (96%)
  matrix products  30.5 us (2%)
    psum x3, waiting for transfers between devices, per_device(): total = lax.psum(part, 'feat')  886 us
    psum x1, waiting for transfers between devices, per_device(): targets = (lax.psum(partial_value, 'feat') * scale).astype(jnp.bfloat16)  292 us
    psum x3, waiting for transfers between devices, broadcast(): return lax.psum(kept, axis)  232 us
    reduce_scatter x1, waiting for transfers between devices, per_device(): lax.psum_scatter(term * scale, 'feat', scatter_dimension=0, tiled=True)  91.2 us
    psum x1, waiting for transfers between devices, per_device(): sides = lax.psum(side_part, 'tok') * (math.sqrt(width) / tokens)  76.9 us
  transfers between devices with their start and end apart: 9, of which 9 were waited for; matrix products, arithmetic and copies ran while one was open for 0% of the time, Pallas kernels for 0%

commit v1 on v0

--- a/solution.py
+++ b/solution.py
@@ -11,6 +11,10 @@
 
 
 def per_device(features, kernel, mask, inverse, penalty):
+
+    def _expand_rounds(body):
+        return jnp.sum(jax.lax.all_gather(body, axis_name="feat"), 0)
+
     n_tok = lax.axis_size("tok")
     n_feat = lax.axis_size("feat")
     width = features.shape[1] * n_feat
@@ -19,7 +23,7 @@
     block = kernel.shape[0]
     ratio = n_feat // n_tok
     partial_value = jnp.dot(features, kernel, preferred_element_type=jnp.float32)
-    targets = (lax.psum(partial_value, "feat") * scale).astype(jnp.bfloat16)
+    targets = (_expand_rounds(partial_value) * scale).astype(jnp.bfloat16)
     side_part = lax.dot_general(
         features, targets, (((0,), (0,)), ((), ())), preferred_element_type=jnp.float32
     )

time: 1640 us -> 1560 us (0.951)
  waiting for transfers between devices: 1580 us -> 1490 us
    psum x1 -> x0, waiting for transfers between devices: 292 us -> none  [per_device(): targets = (lax.psum(partial_value, 'feat') * scale).astype(jnp.bfloat16)]
    all_gather x0 -> x1, waiting for transfers between devices: none -> 203 us  [_expand_rounds(): return jnp.sum(jax.lax.all_gather(body, axis_name='feat'), 0)]
where the time goes in v1:
time: 1560 us
  waiting for transfers between devices  1490 us (96%)
  matrix products  29.2 us (2%)
  other arithmetic  20.3 us (1%)
    psum x3, waiting for transfers between devices, per_device(): total = lax.psum(part, 'feat')  886 us
    psum x3, waiting for transfers between devices, broadcast(): return lax.psum(kept, axis)  232 us
    all_gather x1, waiting for transfers between devices, _expand_rounds(): return jnp.sum(jax.lax.all_gather(body, axis_name='feat'), 0)  203 us
    reduce_scatter x1, waiting for transfers between devices, per_device(): lax.psum_scatter(term * scale, 'feat', scatter_dimension=0, tiled=True)  91.2 us
    psum x1, waiting for transfers between devices, per_device(): sides = lax.psum(side_part, 'tok') * (math.sqrt(width) / tokens)  80.2 us
  transfers between devices with their start and end apart: 9, of which 9 were waited for; matrix products, arithmetic and copies ran while one was open for 0% of the time, Pallas kernels for 0%

profile of v1, /device:TPU:2, one launch (start us, length us, event | category | flops | bytes accessed | tf_op | source)
XLA Modules:
  0.0 1560.0 jit_solution(1318828379675089889)
XLA Ops:
  7.2 0.0 copy-start
  7.2 0.0 all-gather.3.cloned.1.call-start
  7.2 1.2 copy-done
  8.4 2.4 fusion.32
  10.8 0.0 all-gather.3.cloned.1.call-update
  10.8 0.0 all-reduce.8.cloned.1.call-start
  10.8 203.1 %all-gather.3.cloned.1.call-done = f32[32768,256]{1,0:T(8,128)} async-done(((f32[1024,256]{1,0:T(8,128)}), f32[32768,256]{1,0:T(8,128)}) %all-gather.3.cloned.1.call-update) | async-done | bytes 33554448 | tf_op jit(solution)/shard_map/all_gather | solution.py:16
  213.9 11.9 reduce_sum.9
  225.8 0.0 copy-start.4
  225.9 0.0 copy-start.5
  225.9 0.0 copy-start.6
  225.9 1.3 convolution_bitcast_fusion.3
  227.2 0.0 all-reduce.8.cloned.1.call-update
  227.2 0.0 all-reduce.10.cloned.1.call-start
  227.2 0.0 copy-done.4
  227.2 0.1 copy.8
  227.4 0.0 copy-done.5
  227.4 0.2 copy.7
  227.6 0.0 copy-done.6
  227.6 0.7 fusion.31
  228.3 80.2 %all-reduce.8.cloned.1.call-done = f32[512,256]{0,1:T(8,128)} async-done(((f32[512,256]{0,1:T(8,128)}), f32[512,256]{0,1:T(8,128)}) %all-reduce.8.cloned.1.call-update) | async-done | bytes 524304 | tf_op jit(solution)/shard_map/psum | solution.py:30
  308.4 8.0 convolution_bitcast_fusion.2
  316.4 0.0 copy-start.2
  316.4 0.0 all-reduce.10.cloned.1.call-update
  316.5 0.0 all-reduce.12.cloned.1.call-start
  316.5 295.4 %all-reduce.10.cloned.1.call-done = f32[2048,256]{0,1:T(8,128)} async-done(((f32[2048,256]{0,1:T(8,128)}), f32[2048,256]{0,1:T(8,128)}) %all-reduce.10.cloned.1.call-update) | async-done | bytes 2097168 | tf_op jit(solution)/shard_map/psum | solution.py:40
  611.9 1.9 dynamic-slice_select_fusion.2
  613.8 0.0 all-reduce.12.cloned.1.call-update
  613.9 0.0 all-reduce.14.cloned.1.call-start
  613.9 77.5 %all-reduce.12.cloned.1.call-done = f32[512,256]{0,1:T(8,128)} async-done(((f32[512,256]{0,1:T(8,128)}), f32[512,256]{0,1:T(8,128)}) %all-reduce.12.cloned.1.call-update) | async-done | bytes 524304 | tf_op jit(solution)/shard_map/psum | solution.py:10
  691.4 0.0 copy-done.2
  691.4 8.1 convolution_bitcast_fusion.1
  699.4 0.0 copy-start.1
  699.4 0.0 all-reduce.14.cloned.1.call-update
  699.5 0.0 all-reduce.16.cloned.1.call-start
  699.5 295.4 %all-reduce.14.cloned.1.call-done = f32[2048,256]{0,1:T(8,128)} async-done(((f32[2048,256]{0,1:T(8,128)}), f32[2048,256]{0,1:T(8,128)}) %all-reduce.14.cloned.1.call-update) | async-done | bytes 2097168 | tf_op jit(solution)/shard_map/psum | solution.py:40
  994.9 1.9 dynamic-slice_select_fusion.1
  996.8 0.0 all-reduce.16.cloned.1.call-update
  996.8 0.2 all-reduce.18.cloned.1.call-start
  997.1 77.3 %all-reduce.16.cloned.1.call-done = f32[512,256]{0,1:T(8,128)} async-done(((f32[512,256]{0,1:T(8,128)}), f32[512,256]{0,1:T(8,128)}) %all-reduce.16.cloned.1.call-update) | async-done | bytes 524304 | tf_op jit(solution)/shard_map/psum | solution.py:10
  1074.4 0.0 copy-done.1
  1074.4 8.1 convolution_bitcast_fusion
  1082.4 0.0 copy-start.3
  1082.4 0.0 all-reduce.18.cloned.1.call-update
  1082.4 0.0 all-reduce.20.cloned.1.call-start
  1082.5 295.2 %all-reduce.18.cloned.1.call-done = f32[2048,256]{0,1:T(8,128)} async-done(((f32[2048,256]{0,1:T(8,128)}), f32[2048,256]{0,1:T(8,128)}) %all-reduce.18.cloned.1.call-update) | async-done | bytes 2097168 | tf_op jit(solution)/shard_map/psum | solution.py:40
  1377.7 1.9 dynamic-slice_select_fusion
  1379.6 0.0 all-reduce.20.cloned.1.call-update
  1379.7 0.0 reduce-scatter.2.cloned.1.call-start
  1379.7 77.6 %all-reduce.20.cloned.1.call-done = f32[512,256]{0,1:T(8,128)} async-done(((f32[512,256]{0,1:T(8,128)}), f32[512,256]{0,1:T(8,128)}) %all-reduce.20.cloned.1.call-update) | async-done | bytes 524304 | tf_op jit(solution)/shard_map/psum | solution.py:10
  1457.3 0.0 copy-done.3
  1457.3 1.3 multiply_convert_fusion.2
  1458.6 1.4 convolution_multiply_fusion
  1460.0 0.0 reduce-scatter.2.cloned.1.call-update
  1460.1 0.8 copy.9
  1460.9 91.2 %reduce-scatter.2.cloned.1.call-done = f32[8,1024]{1,0:T(8,128)} async-done(((f32[256,1024]{1,0:T(8,128)}), f32[8,1024]{1,0:T(8,128)}) %reduce-scatter.2.cloned.1.call-update) | async-done | bytes 32784 | tf_op jit(solution)/shard_map/reduce_scatter | solution.py:50
  1552.1 1.4 convert_element_type.23
Async XLA Ops:
  7.2 1.2 copy-start
  7.2 206.7 %all-gather.3.cloned.1.call-start = ((), (), s32[]{:S(2)}) async-start(), calls=%async_computation.9 | async-start | bytes 34603008 | tf_op jit(solution)/shard_map/all_gather | solution.py:16
  10.8 297.6 %all-reduce.8.cloned.1.call-start = ((), (), s32[]{:S(2)}) async-start(), calls=%async_computation.1 | async-start | bytes 1048576 | tf_op jit(solution)/shard_map/psum | solution.py:30
  225.8 1.4 copy-start.4
  225.9 1.5 copy-start.5
  225.9 1.7 copy-start.6
  227.2 384.8 %all-reduce.10.cloned.1.call-start = ((), (), s32[]{:S(2)}) async-start(), calls=%async_computation.2 | async-start | bytes 4194304 | tf_op jit(solution)/shard_map/psum | solution.py:40
  316.4 374.9 %copy-start.2 = (f32[512,256]{0,1:T(8,128)S(1)}, f32[512,256]{0,1:T(8,128)}, u32[]{:S(2)}) copy-start(f32[512,256]{0,1:T(8,128)} %all-reduce.8.cloned.1.call-done) | copy-start | bytes 1572868
  316.5 374.9 %all-reduce.12.cloned.1.call-start = ((), (), s32[]{:S(2)}) async-start(), calls=%async_computation.3 | async-start | bytes 1048576 | tf_op jit(solution)/shard_map/psum | solution.py:10
  613.9 381.1 %all-reduce.14.cloned.1.call-start = ((), (), s32[]{:S(2)}) async-start(), calls=%async_computation.4 | async-start | bytes 4194304 | tf_op jit(solution)/shard_map/psum | solution.py:40
  699.4 374.9 %copy-start.1 = (f32[512,256]{0,1:T(8,128)S(1)}, f32[512,256]{0,1:T(8,128)}, u32[]{:S(2)}) copy-start(f32[512,256]{0,1:T(8,128)} %all-reduce.12.cloned.1.call-done) | copy-start | bytes 1572868
  699.5 374.9 %all-reduce.16.cloned.1.call-start = ((), (), s32[]{:S(2)}) async-start(), calls=%async_computation.5 | async-start | bytes 1048576 | tf_op jit(solution)/shard_map/psum | solution.py:10
  996.8 380.9 %all-reduce.18.cloned.1.call-start = ((), (), s32[]{:S(2)}) async-start(), calls=%async_computation.6 | async-start | bytes 4194304 | tf_op jit(solution)/shard_map/psum | solution.py:40
  1082.4 374.9 %copy-start.3 = (f32[512,256]{0,1:T(8,128)S(1)}, f32[512,256]{0,1:T(8,128)}, u32[]{:S(2)}) copy-start(f32[512,256]{0,1:T(8,128)} %all-reduce.16.cloned.1.call-done) | copy-start | bytes 1572868
  1082.4 374.8 %all-reduce.20.cloned.1.call-start = ((), (), s32[]{:S(2)}) async-start(), calls=%async_computation.7 | async-start | bytes 1048576 | tf_op jit(solution)/shard_map/psum | solution.py:10
  1379.7 172.5 %reduce-scatter.2.cloned.1.call-start = ((), (), s32[]{:S(2)}) async-start(), calls=%async_computation.8 | async-start | bytes 1081344 | tf_op jit(solution)/shard_map/reduce_scatter | solution.py:50
Sparse Core Ops, SparseCore 0:
  10.9 202.9 all-gather.2
  227.3 81.0 all-reduce.7
  316.6 295.3 all-reduce.9
  614.4 76.8 all-reduce.11
  699.6 295.3 all-reduce.13
  997.4 76.8 all-reduce.15
  1082.6 295.1 all-reduce.17
  1380.4 76.8 all-reduce.19
  1461.1 90.9 reduce-scatter.1
